TPU v7x, 32 devices: a whole 2x2x4 slice. The times are simulated.
32 devices in a mesh: chan: 4 (over y, x), blk: 8 (over z, core).
Axes of the slice: x: 2, y: 2, z: 4, core: 2. Of those that a mesh axis runs over, the one named last changes fastest.
Arguments:
- coeffs: bfloat16 [12, 2, 3072, 1536], P('chan', None, 'blk'), may hold values from -0.15 to 0.15
- legendre: bfloat16 [4, 768, 256, 1536], P('chan', 'blk'), may hold values from -0.15625 to 0.15625
- m_order: int32 [3072], replicated, may hold values from 0 to 3071, as said below
- sector_len: int32 [512, 16], P(('chan', 'blk')), may hold values from 256 to 4352, as said below
Outputs:
- ilc_map: float32 [512, 8192], P(('chan', 'blk'))
Inputs may be any that keep to these rules, and one draw needn't show every extreme that they name: `m_order`: a permutation of 0 to 3071; slots 2 j and 2 j + 1 hold the orders m and 3071 - m. `sector_len`: the 16 lengths of each cycle sum to 8192.
All inputs are finite; a program needn't handle non-finite values.
Results may differ from a plain program's by a relative error of at most 0.0003.
Values may be sent and summed in bfloat16 or wider, within the bound.
A program may use at most 512 MiB of HBM per device.

v0:
```python
import jax
import jax.numpy as jnp
from jax import lax
from jax.sharding import PartitionSpec as P

M = 3072
LB = 1536
PIX = 8192
RIDGE_FACTOR = 0.05
TWO_PI = 6.283185307179586


def cycle_synthesis(spectra, orders):
    highest = lax.Precision.HIGHEST
    order_count = spectra.shape[-1]
    fine_count = 128
    coarse_count = PIX // fine_count
    coarse_phase = (lax.iota(jnp.int32, coarse_count) * fine_count)[:, None] * orders[None, :] % PIX
    fine_phase = orders[:, None] * lax.iota(jnp.int32, fine_count)[None, :] % PIX
    coarse_angle = coarse_phase.astype(jnp.float32) * (TWO_PI / PIX)
    fine_angle = fine_phase.astype(jnp.float32) * (TWO_PI / PIX)
    weight = jnp.where(orders == 0, 1.0, 2.0).astype(jnp.float32)
    coarse_cos = jnp.cos(coarse_angle)
    coarse_sin = jnp.sin(coarse_angle)
    fine_cos = weight[:, None] * jnp.cos(fine_angle)
    fine_sin = weight[:, None] * jnp.sin(fine_angle)
    real_part = spectra[:, 0].reshape(-1, 1, order_count)
    imag_part = spectra[:, 1].reshape(-1, 1, order_count)
    shifted_real = (real_part * coarse_cos[None] - imag_part * coarse_sin[None]).reshape(
        -1, order_count
    )
    shifted_imag = (real_part * coarse_sin[None] + imag_part * coarse_cos[None]).reshape(
        -1, order_count
    )
    result = jnp.dot(shifted_real, fine_cos, precision=highest, preferred_element_type=jnp.float32)
    result = result - jnp.dot(
        shifted_imag, fine_sin, precision=highest, preferred_element_type=jnp.float32
    )
    return result.reshape(spectra.shape[0], spectra.shape[2], PIX)


def cycle_combine(cycle_map, lengths):
    highest = lax.Precision.HIGHEST
    channel_count = cycle_map.shape[0]
    sector_end = jnp.cumsum(lengths)
    sector_start = sector_end - lengths
    pixels = lax.iota(jnp.int32, PIX)
    member = (
        (pixels[None, :] >= sector_start[:, None]) & (pixels[None, :] < sector_end[:, None])
    ).astype(jnp.float32)
    products = (cycle_map[:, None, :] * cycle_map[None, :, :]).reshape(
        channel_count * channel_count, PIX
    )
    moments = jnp.einsum("qx,kx->kq", products, member, precision=highest)
    covariance = (
        moments.reshape(-1, channel_count, channel_count)
        / lengths.astype(jnp.float32)[:, None, None]
    )
    trace_part = jnp.trace(covariance, axis1=1, axis2=2) * (RIDGE_FACTOR / channel_count)
    regular = covariance + trace_part[:, None, None] * jnp.eye(channel_count, dtype=jnp.float32)
    factor = jnp.linalg.cholesky(regular)
    unit_rhs = jnp.ones((covariance.shape[0], channel_count, 1), jnp.float32)
    forward = lax.linalg.triangular_solve(factor, unit_rhs, left_side=True, lower=True)
    solved = lax.linalg.triangular_solve(
        factor, forward, left_side=True, lower=True, transpose_a=True
    )[:, :, 0]
    weights = solved / jnp.sum(solved, axis=1, keepdims=True)
    pixel_weights = jnp.einsum("ka,kx->ax", weights, member, precision=highest)
    return jnp.sum(pixel_weights * cycle_map, axis=0)


def per_device(coeffs, legendre, m_order, sector_len):
    slot_count = legendre.shape[1]
    group_count = lax.axis_size("chan")
    block_count = lax.axis_size("blk")
    first_slot = (lax.axis_index("blk") * group_count + lax.axis_index("chan")) * slot_count
    orders = lax.dynamic_slice_in_dim(m_order, first_slot, slot_count, 0)
    operator = legendre[0]
    degree = M - LB + lax.iota(jnp.int32, LB)
    valid_mask = degree[None, :] >= orders[:, None]
    zero_value = jnp.zeros((), coeffs.dtype)
    coeff_part = lax.all_to_all(coeffs, "chan", split_axis=2, concat_axis=0, tiled=True)
    odd_mask = (degree[None, :] + orders[:, None]) % 2 == 1
    even_part = jnp.where((valid_mask & ~odd_mask)[None, None], coeff_part, zero_value)
    odd_part = jnp.where((valid_mask & odd_mask)[None, None], coeff_part, zero_value)
    even_sum = jnp.einsum("cpsl,srl->cprs", even_part, operator, preferred_element_type=jnp.float32)
    odd_sum = jnp.einsum("cpsl,srl->cprs", odd_part, operator, preferred_element_type=jnp.float32)
    spectra = jnp.concatenate([even_sum + odd_sum, even_sum - odd_sum], axis=2)
    order_joined = (
        m_order.reshape(block_count, group_count, slot_count).transpose(1, 0, 2).reshape(-1)
    )
    cycle_maps = (lambda spectrum: cycle_synthesis(spectrum, order_joined))(
        lax.all_to_all(spectra, ("chan", "blk"), split_axis=2, concat_axis=3, tiled=True)
    )
    return lax.map(
        lambda cycle_pair: cycle_combine(cycle_pair[0], cycle_pair[1]),
        (jnp.moveaxis(cycle_maps, 1, 0), sector_len),
    )


def solution(mesh):
    placed = (
        P("chan", None, "blk", None),
        P("chan", "blk", None, None),
        P(),
        P(("chan", "blk"), None),
    )
    return jax.shard_map(
        per_device, mesh=mesh, in_specs=placed, out_specs=P(("chan", "blk"), None), check_vma=False
    )
```

profile of v0, /device:TPU:0, one launch (start us, length us, event | category | flops | bytes accessed | tf_op | source)
XLA Modules:
  0.0 1442.0 jit_solution(16301609392654005439)
XLA Ops:
  0.0 11.6 copy.69
  18.2 104.5 %all-to-all-done = bf16[3,2,384,1536]{3,0,1,2:T(4,128)(2,1)} async-done(((bf16[3,2,384,1536]{3,0,1,2:T(4,128)(2,1)}), bf16[3,2,384,1536]{3,0,1,2:T(4,128)(2,1)}, u32[]{:S(2)}, u32[]{:S(2)}) %all-to-all-start) | async-done | bytes 7077920 | tf_op jit(solution)/shard_map/all_to_all | solution.py:82
  132.6 10.2 bitcast_select_fusion
  142.8 33.3 %fusion.23 = f32[96,12,2,256]{3,1,2,0:T(8,128)S(1)} fusion(bf16[1,96,256,1536]{3,2,1,0:T(8,128)(2,1)} %param.7, bf16[12,2,96,1536]{3,2,1,0:T(8,128)(2,1)} %get-tuple-element.40), kind=kOutput, calls=%fused_computation.41 | convolution fusion | flops 1811939328 | bytes 84934656 | tf_op jit(solution)/shard_map/cpsl,srl->cprs/dot_general | solution.py:87
  176.1 34.2 %add_bitcast_fusion = (f32[12,2,256,96]{2,0,1,3:T(8,128)}, f32[12,2,256,96]{2,0,1,3:T(8,128)}) fusion(f32[96,12,2,256]{3,1,2,0:T(8,128)S(1)} %fusion.23, bf16[1,96,256,1536]{3,2,1,0:T(8,128)(2,1)} %param.7, bf16[12,2,96,1536]{3,2,1,0:T(8,128)(2,1)} %get-tuple-element.41), kind=kOutput, calls=%fused_computation.53 | convolution fusion | flops 1813118976 | bytes 89653248 | tf_op jit(solution)/shard_map/cpsl,srl->cprs/dot_general | solution.py:86
  217.0 9.7 copy.74
  236.3 8.1 fusion.76
  244.4 8.1 fusion.74
  252.4 119.3 %all-to-all-done.1 = f32[12,2,512,96]{3,1,0,2:T(2,128)} async-done(((f32[12,2,512,96]{3,1,0,2:T(2,128)}), f32[12,2,512,96]{3,1,0,2:T(2,128)}, u32[]{:S(2)}, u32[]{:S(2)}) %all-to-all-start.1) | async-done | bytes 4718624 | tf_op jit(solution)/shard_map/all_to_all | solution.py:93
  380.8 7.7 all_to_all.33
  391.4 95.4 %multiply_add_fusion = (f32[192,64,3072]{2,1,0:T(8,128)}, f32[192,64,3072]{2,1,0:T(8,128)}) fusion(f32[64,3072]{1,0:T(8,128)} %get-tuple-element.49, f32[192,3072]{1,0:T(8,128)S(1)} %bitcast.106, f32[64,3072]{1,0:T(8,128)} %get-tuple-element.48, f32[192,3072]{1,0:T(8,128)S(1)} %bitcast.105), kind=kLoop, calls=%fused_computation.39 | loop fusion | flops 226492416 | bytes 308281344 | tf_op jit(solution)/shard_map/add | solution.py:32
  486.8 126.1 %fusion.34 = f32[12288,128]{1,0:T(8,128)} fusion(f32[12288,3072]{1,0:T(8,128)} %bitcast.29, f32[3072,128]{1,0:T(8,128)} %fusion.76), kind=kOutput, calls=%fused_computation.62 | convolution fusion | flops 57982058496 | bytes 158859264 | tf_op jit(solution)/shard_map/dot_general | solution.py:35
  612.9 125.4 %convolution_subtract_fusion = f32[12288,128]{1,0:T(8,128)} fusion(f32[12288,128]{1,0:T(8,128)} %fusion.34, f32[12288,3072]{1,0:T(8,128)} %bitcast.30, f32[3072,128]{1,0:T(8,128)S(1)} %copy-done), kind=kOutput, calls=%fused_computation.45 | convolution fusion | flops 57983631360 | bytes 165150720 | tf_op jit(solution)/shard_map/dot_general | solution.py:36
  738.3 7.4 reshape.296
  745.7 9.7 copy.91
  755.4 686.4 %while.10 = (s32[]{:T(128)}, f32[16,8192]{1,0:T(8,128)}, s32[16,16]{1,0:T(8,128)}, f32[16,12,8192]{2,1,0:T(8,128)}, s32[]{:T(128)}, /*index=5*/s32[]{:T(128)}, f32[]{:T(128)}, f32[]{:T(128)}) while((s32[]{:T(128)}, f32[16,8192]{1,0:T(8,128)}, s32[16,16]{1,0:T(8,128)}, f32[16,12,8192]{2,1,0:T(8,128)}, s32[]{:T(128)}, /*index=5*/s32[]{:T(128)}, ...), condition=%wide.region_7.8_spmd, body=%wide.region_0.7_spmd.sunk | while | flops 247610512 | bytes 1840549 | solution.py:95
  762.4 17.6 %custom-call.12 = f32[16,12,12]{2,1,0:T(8,128)S(1)} custom-call(f32[16,12,12]{2,1,0:T(8,128)S(1)} %copy.101), custom_call_target="Cholesky" | custom-call | tf_op jit(solution)/shard_map/while/body/eval_jaxpr/jit(cholesky)/cholesky | solution.py:61
  780.3 14.9 %custom-call.13 = f32[16,1,12,12]{2,3,1,0:T(8,128)S(1)} custom-call(f32[16,1,12,12]{3,2,1,0:T(8,128)S(1)} %select_bitcast_fusion.2), custom_call_target="InvertDiagBlocksLowerTriangular" | custom-call | tf_op jit(solution)/shard_map/while/body/eval_jaxpr/triangular_solve | solution.py:64
  805.3 17.6 %custom-call.12 = f32[16,12,12]{2,1,0:T(8,128)S(1)} custom-call(f32[16,12,12]{2,1,0:T(8,128)S(1)} %copy.101), custom_call_target="Cholesky" | custom-call | tf_op jit(solution)/shard_map/while/body/eval_jaxpr/jit(cholesky)/cholesky | solution.py:61
  823.2 14.9 %custom-call.13 = f32[16,1,12,12]{2,3,1,0:T(8,128)S(1)} custom-call(f32[16,1,12,12]{3,2,1,0:T(8,128)S(1)} %select_bitcast_fusion.2), custom_call_target="InvertDiagBlocksLowerTriangular" | custom-call | tf_op jit(solution)/shard_map/while/body/eval_jaxpr/triangular_solve | solution.py:64
  848.2 17.6 %custom-call.12 = f32[16,12,12]{2,1,0:T(8,128)S(1)} custom-call(f32[16,12,12]{2,1,0:T(8,128)S(1)} %copy.101), custom_call_target="Cholesky" | custom-call | tf_op jit(solution)/shard_map/while/body/eval_jaxpr/jit(cholesky)/cholesky | solution.py:61
  866.1 14.9 %custom-call.13 = f32[16,1,12,12]{2,3,1,0:T(8,128)S(1)} custom-call(f32[16,1,12,12]{3,2,1,0:T(8,128)S(1)} %select_bitcast_fusion.2), custom_call_target="InvertDiagBlocksLowerTriangular" | custom-call | tf_op jit(solution)/shard_map/while/body/eval_jaxpr/triangular_solve | solution.py:64
  891.1 17.6 %custom-call.12 = f32[16,12,12]{2,1,0:T(8,128)S(1)} custom-call(f32[16,12,12]{2,1,0:T(8,128)S(1)} %copy.101), custom_call_target="Cholesky" | custom-call | tf_op jit(solution)/shard_map/while/body/eval_jaxpr/jit(cholesky)/cholesky | solution.py:61
  909.0 14.9 %custom-call.13 = f32[16,1,12,12]{2,3,1,0:T(8,128)S(1)} custom-call(f32[16,1,12,12]{3,2,1,0:T(8,128)S(1)} %select_bitcast_fusion.2), custom_call_target="InvertDiagBlocksLowerTriangular" | custom-call | tf_op jit(solution)/shard_map/while/body/eval_jaxpr/triangular_solve | solution.py:64
  934.0 17.6 %custom-call.12 = f32[16,12,12]{2,1,0:T(8,128)S(1)} custom-call(f32[16,12,12]{2,1,0:T(8,128)S(1)} %copy.101), custom_call_target="Cholesky" | custom-call | tf_op jit(solution)/shard_map/while/body/eval_jaxpr/jit(cholesky)/cholesky | solution.py:61
  951.9 14.9 %custom-call.13 = f32[16,1,12,12]{2,3,1,0:T(8,128)S(1)} custom-call(f32[16,1,12,12]{3,2,1,0:T(8,128)S(1)} %select_bitcast_fusion.2), custom_call_target="InvertDiagBlocksLowerTriangular" | custom-call | tf_op jit(solution)/shard_map/while/body/eval_jaxpr/triangular_solve | solution.py:64
  976.9 17.6 %custom-call.12 = f32[16,12,12]{2,1,0:T(8,128)S(1)} custom-call(f32[16,12,12]{2,1,0:T(8,128)S(1)} %copy.101), custom_call_target="Cholesky" | custom-call | tf_op jit(solution)/shard_map/while/body/eval_jaxpr/jit(cholesky)/cholesky | solution.py:61
  994.8 14.9 %custom-call.13 = f32[16,1,12,12]{2,3,1,0:T(8,128)S(1)} custom-call(f32[16,1,12,12]{3,2,1,0:T(8,128)S(1)} %select_bitcast_fusion.2), custom_call_target="InvertDiagBlocksLowerTriangular" | custom-call | tf_op jit(solution)/shard_map/while/body/eval_jaxpr/triangular_solve | solution.py:64
  1019.8 17.6 %custom-call.12 = f32[16,12,12]{2,1,0:T(8,128)S(1)} custom-call(f32[16,12,12]{2,1,0:T(8,128)S(1)} %copy.101), custom_call_target="Cholesky" | custom-call | tf_op jit(solution)/shard_map/while/body/eval_jaxpr/jit(cholesky)/cholesky | solution.py:61
  1037.7 14.9 %custom-call.13 = f32[16,1,12,12]{2,3,1,0:T(8,128)S(1)} custom-call(f32[16,1,12,12]{3,2,1,0:T(8,128)S(1)} %select_bitcast_fusion.2), custom_call_target="InvertDiagBlocksLowerTriangular" | custom-call | tf_op jit(solution)/shard_map/while/body/eval_jaxpr/triangular_solve | solution.py:64
  1062.7 17.6 %custom-call.12 = f32[16,12,12]{2,1,0:T(8,128)S(1)} custom-call(f32[16,12,12]{2,1,0:T(8,128)S(1)} %copy.101), custom_call_target="Cholesky" | custom-call | tf_op jit(solution)/shard_map/while/body/eval_jaxpr/jit(cholesky)/cholesky | solution.py:61
  1080.6 14.9 %custom-call.13 = f32[16,1,12,12]{2,3,1,0:T(8,128)S(1)} custom-call(f32[16,1,12,12]{3,2,1,0:T(8,128)S(1)} %select_bitcast_fusion.2), custom_call_target="InvertDiagBlocksLowerTriangular" | custom-call | tf_op jit(solution)/shard_map/while/body/eval_jaxpr/triangular_solve | solution.py:64
  1105.6 17.6 %custom-call.12 = f32[16,12,12]{2,1,0:T(8,128)S(1)} custom-call(f32[16,12,12]{2,1,0:T(8,128)S(1)} %copy.101), custom_call_target="Cholesky" | custom-call | tf_op jit(solution)/shard_map/while/body/eval_jaxpr/jit(cholesky)/cholesky | solution.py:61
  1123.5 14.9 %custom-call.13 = f32[16,1,12,12]{2,3,1,0:T(8,128)S(1)} custom-call(f32[16,1,12,12]{3,2,1,0:T(8,128)S(1)} %select_bitcast_fusion.2), custom_call_target="InvertDiagBlocksLowerTriangular" | custom-call | tf_op jit(solution)/shard_map/while/body/eval_jaxpr/triangular_solve | solution.py:64
  1148.5 17.6 %custom-call.12 = f32[16,12,12]{2,1,0:T(8,128)S(1)} custom-call(f32[16,12,12]{2,1,0:T(8,128)S(1)} %copy.101), custom_call_target="Cholesky" | custom-call | tf_op jit(solution)/shard_map/while/body/eval_jaxpr/jit(cholesky)/cholesky | solution.py:61
  1166.4 14.9 %custom-call.13 = f32[16,1,12,12]{2,3,1,0:T(8,128)S(1)} custom-call(f32[16,1,12,12]{3,2,1,0:T(8,128)S(1)} %select_bitcast_fusion.2), custom_call_target="InvertDiagBlocksLowerTriangular" | custom-call | tf_op jit(solution)/shard_map/while/body/eval_jaxpr/triangular_solve | solution.py:64
  1191.4 17.6 %custom-call.12 = f32[16,12,12]{2,1,0:T(8,128)S(1)} custom-call(f32[16,12,12]{2,1,0:T(8,128)S(1)} %copy.101), custom_call_target="Cholesky" | custom-call | tf_op jit(solution)/shard_map/while/body/eval_jaxpr/jit(cholesky)/cholesky | solution.py:61
  1209.3 14.9 %custom-call.13 = f32[16,1,12,12]{2,3,1,0:T(8,128)S(1)} custom-call(f32[16,1,12,12]{3,2,1,0:T(8,128)S(1)} %select_bitcast_fusion.2), custom_call_target="InvertDiagBlocksLowerTriangular" | custom-call | tf_op jit(solution)/shard_map/while/body/eval_jaxpr/triangular_solve | solution.py:64
  1234.3 17.6 %custom-call.12 = f32[16,12,12]{2,1,0:T(8,128)S(1)} custom-call(f32[16,12,12]{2,1,0:T(8,128)S(1)} %copy.101), custom_call_target="Cholesky" | custom-call | tf_op jit(solution)/shard_map/while/body/eval_jaxpr/jit(cholesky)/cholesky | solution.py:61
  1252.2 14.9 %custom-call.13 = f32[16,1,12,12]{2,3,1,0:T(8,128)S(1)} custom-call(f32[16,1,12,12]{3,2,1,0:T(8,128)S(1)} %select_bitcast_fusion.2), custom_call_target="InvertDiagBlocksLowerTriangular" | custom-call | tf_op jit(solution)/shard_map/while/body/eval_jaxpr/triangular_solve | solution.py:64
  1277.2 17.6 %custom-call.12 = f32[16,12,12]{2,1,0:T(8,128)S(1)} custom-call(f32[16,12,12]{2,1,0:T(8,128)S(1)} %copy.101), custom_call_target="Cholesky" | custom-call | tf_op jit(solution)/shard_map/while/body/eval_jaxpr/jit(cholesky)/cholesky | solution.py:61
  1295.1 14.9 %custom-call.13 = f32[16,1,12,12]{2,3,1,0:T(8,128)S(1)} custom-call(f32[16,1,12,12]{3,2,1,0:T(8,128)S(1)} %select_bitcast_fusion.2), custom_call_target="InvertDiagBlocksLowerTriangular" | custom-call | tf_op jit(solution)/shard_map/while/body/eval_jaxpr/triangular_solve | solution.py:64
  1320.1 17.6 %custom-call.12 = f32[16,12,12]{2,1,0:T(8,128)S(1)} custom-call(f32[16,12,12]{2,1,0:T(8,128)S(1)} %copy.101), custom_call_target="Cholesky" | custom-call | tf_op jit(solution)/shard_map/while/body/eval_jaxpr/jit(cholesky)/cholesky | solution.py:61
  1338.0 14.9 %custom-call.13 = f32[16,1,12,12]{2,3,1,0:T(8,128)S(1)} custom-call(f32[16,1,12,12]{3,2,1,0:T(8,128)S(1)} %select_bitcast_fusion.2), custom_call_target="InvertDiagBlocksLowerTriangular" | custom-call | tf_op jit(solution)/shard_map/while/body/eval_jaxpr/triangular_solve | solution.py:64
  1363.0 17.6 %custom-call.12 = f32[16,12,12]{2,1,0:T(8,128)S(1)} custom-call(f32[16,12,12]{2,1,0:T(8,128)S(1)} %copy.101), custom_call_target="Cholesky" | custom-call | tf_op jit(solution)/shard_map/while/body/eval_jaxpr/jit(cholesky)/cholesky | solution.py:61
  1380.9 14.9 %custom-call.13 = f32[16,1,12,12]{2,3,1,0:T(8,128)S(1)} custom-call(f32[16,1,12,12]{3,2,1,0:T(8,128)S(1)} %select_bitcast_fusion.2), custom_call_target="InvertDiagBlocksLowerTriangular" | custom-call | tf_op jit(solution)/shard_map/while/body/eval_jaxpr/triangular_solve | solution.py:64
  1405.9 17.6 %custom-call.12 = f32[16,12,12]{2,1,0:T(8,128)S(1)} custom-call(f32[16,12,12]{2,1,0:T(8,128)S(1)} %copy.101), custom_call_target="Cholesky" | custom-call | tf_op jit(solution)/shard_map/while/body/eval_jaxpr/jit(cholesky)/cholesky | solution.py:61
  1423.8 14.9 %custom-call.13 = f32[16,1,12,12]{2,3,1,0:T(8,128)S(1)} custom-call(f32[16,1,12,12]{3,2,1,0:T(8,128)S(1)} %select_bitcast_fusion.2), custom_call_target="InvertDiagBlocksLowerTriangular" | custom-call | tf_op jit(solution)/shard_map/while/body/eval_jaxpr/triangular_solve | solution.py:64
  (454 shorter events, 210.3 us)
Async XLA Ops:
  11.6 6.0 copy-start.1
  11.6 111.1 %all-to-all-start = ((bf16[3,2,384,1536]{3,0,1,2:T(4,128)(2,1)}), bf16[3,2,384,1536]{3,0,1,2:T(4,128)(2,1)}, u32[]{:S(2)}, u32[]{:S(2)}) async-start(bf16[3,2,384,1536]{3,0,1,2:T(4,128)(2,1)} %copy.69), calls=%async_computation | async-start | bytes 18874368 | tf_op jit(solution)/shard_map/all_to_all | solution.py:82
  226.7 145.1 %all-to-all-start.1 = ((f32[12,2,512,96]{3,1,0,2:T(2,128)}), f32[12,2,512,96]{3,1,0,2:T(2,128)}, u32[]{:S(2)}, u32[]{:S(2)}) async-start(f32[12,2,512,96]{3,1,0,2:T(2,128)} %copy.74), calls=%async_computation.1 | async-start | bytes 12582912 | tf_op jit(solution)/shard_map/all_to_all | solution.py:93
  486.8 126.1 %copy-start = (f32[3072,128]{1,0:T(8,128)S(1)}, f32[3072,128]{1,0:T(8,128)}, u32[]{:S(2)}) copy-start(f32[3072,128]{1,0:T(8,128)} %fusion.74) | copy-start | bytes 4718596
where the time goes:
time: 1450 us; the launch traced here: 1440 us
  other arithmetic  690 us (48%)
  matrix products  390 us (27%)
  waiting for transfers between devices  224 us (15%)
  local copies, waits for them, and re-layouts  126 us (9%)
    another operation x64, other arithmetic, cycle_combine(): factor = jnp.linalg.cholesky(regular)  284 us
    another operation x48, other arithmetic, cycle_combine(): lax.linalg.triangular_solve(factor, forward, left_side=True, lower=True,...  240 us
    dot_general x1, matrix products, cycle_synthesis(): jnp.dot(shifted_real, fine_cos, precision=highest, preferred_element_type...  126 us
    dot_general x1, matrix products, cycle_synthesis(): jnp.dot(shifted_imag, fine_sin, precision=highest, preferred_element_type...  125 us
    all_to_all x1, waiting for transfers between devices, per_device(): lax.all_to_all(spectra, ('chan', 'blk'), split_axis=2, concat_axis=3, til...  119 us
    all_to_all x1, waiting for transfers between devices, per_device(): lax.all_to_all(coeffs, 'chan', split_axis=2, concat_axis=0, tiled=True)  105 us
    add x1, other arithmetic, cycle_synthesis(): real_part * coarse_sin[None] + imag_part * coarse_cos[None]  95.4 us
    dot_general x16, matrix products, cycle_combine(): moments = jnp.einsum('qx,kx->kq', products, member, precision=highest)  51.2 us
  transfers between devices with their start and end apart: 2, of which 2 were waited for; matrix products, arithmetic and copies ran while one was open for 1% of the time, Pallas kernels for 0%

commit v1 on v0

--- a/solution.py
+++ b/solution.py
@@ -90,7 +90,15 @@
         m_order.reshape(block_count, group_count, slot_count).transpose(1, 0, 2).reshape(-1)
     )
     cycle_maps = (lambda spectrum: cycle_synthesis(spectrum, order_joined))(
-        lax.all_to_all(spectra, ("chan", "blk"), split_axis=2, concat_axis=3, tiled=True)
+        jnp.concatenate(
+            lax.all_to_all(
+                jnp.stack(jnp.split(spectra, lax.axis_size(("chan", "blk")), axis=2)),
+                ("chan", "blk"),
+                0,
+                0,
+            ),
+            axis=3,
+        )
     )
     return lax.map(
         lambda cycle_pair: cycle_combine(cycle_pair[0], cycle_pair[1]),

time: 1450 us -> 1590 us (1.097)
  local copies, waits for them, and re-layouts: 126 us -> 268 us
    another operation x32 -> x67, local copies, waits for them, and re-layouts: 1.38 us -> 120 us  [the longest x35 119 us: per_device(): jnp.stack(jnp.split(spectra, lax.axis_size(('chan', 'blk')), axis=2))]
    unnamed x5 -> x74, local copies, waits for them, and re-layouts: 11.6 us -> 45.3 us
    reshape x0 -> x2, local copies, waits for them, and re-layouts: none -> 16.7 us  [per_device(): jnp.concatenate(lax.all_to_all(jnp.stack(jnp.split(spectra, lax.axis_size...]
    all_to_all x3 -> x0, local copies, waits for them, and re-layouts: 16.7 us -> none  [per_device(): lax.all_to_all(spectra, ('chan', 'blk'), split_axis=2, concat_axis=3, til...]
where the time goes in v1:
time: 1590 us; the launch traced here: 1580 us
  other arithmetic  683 us (43%)
  matrix products  387 us (24%)
  local copies, waits for them, and re-layouts  268 us (17%)
  waiting for transfers between devices  224 us (14%)
    another operation x64, other arithmetic, cycle_combine(): factor = jnp.linalg.cholesky(regular)  284 us
    another operation x48, other arithmetic, cycle_combine(): lax.linalg.triangular_solve(factor, forward, left_side=True, lower=True,...  240 us
    dot_general x1, matrix products, cycle_synthesis(): jnp.dot(shifted_real, fine_cos, precision=highest, preferred_element_type...  126 us
    dot_general x1, matrix products, cycle_synthesis(): jnp.dot(shifted_imag, fine_sin, precision=highest, preferred_element_type...  125 us
    all_to_all x1, waiting for transfers between devices, per_device(): lax.all_to_all(jnp.stack(jnp.split(spectra, lax.axis_size(('chan', 'blk')...  119 us
    another operation x35, local copies, waits for them, and re-layouts, per_device(): jnp.stack(jnp.split(spectra, lax.axis_size(('chan', 'blk')), axis=2))  119 us
    all_to_all x1, waiting for transfers between devices, per_device(): lax.all_to_all(coeffs, 'chan', split_axis=2, concat_axis=0, tiled=True)  104 us
    add x1, other arithmetic, cycle_synthesis(): real_part * coarse_sin[None] + imag_part * coarse_cos[None]  95.4 us
  transfers between devices with their start and end apart: 2, of which 2 were waited for; matrix products, arithmetic and copies ran while one was open for 1% of the time, Pallas kernels for 0%

profile of v1, /device:TPU:0, one launch (start us, length us, event | category | flops | bytes accessed | tf_op | source)
XLA Modules:
  0.0 1576.1 jit_solution(16239727196051832581)
XLA Ops:
  0.0 11.6 copy.131
  18.2 104.5 %all-to-all-done = bf16[3,2,384,1536]{3,0,1,2:T(4,128)(2,1)} async-done(((bf16[3,2,384,1536]{3,0,1,2:T(4,128)(2,1)}), bf16[3,2,384,1536]{3,0,1,2:T(4,128)(2,1)}, u32[]{:S(2)}, u32[]{:S(2)}) %all-to-all-start) | async-done | bytes 7077920 | tf_op jit(solution)/shard_map/all_to_all | solution.py:82
  132.5 10.2 bitcast_select_fusion
  142.6 32.4 %fusion.23 = f32[96,12,2,256]{3,1,2,0:T(8,128)} fusion(bf16[1,96,256,1536]{3,2,1,0:T(8,128)(2,1)} %param.7, bf16[12,2,96,1536]{3,2,1,0:T(8,128)(2,1)} %get-tuple-element.40), kind=kOutput, calls=%fused_computation.41 | convolution fusion | flops 1811939328 | bytes 84934656 | tf_op jit(solution)/shard_map/cpsl,srl->cprs/dot_general | solution.py:87
  175.0 32.9 %subtract_bitcast_fusion = (f32[12,2,256,96]{2,0,1,3:T(8,128)S(1)}, f32[12,2,256,96]{2,0,1,3:T(8,128)}) fusion(f32[96,12,2,256]{3,1,2,0:T(8,128)} %fusion.23, bf16[1,96,256,1536]{3,2,1,0:T(8,128)(2,1)} %param.7, bf16[12,2,96,1536]{3,2,1,0:T(8,128)(2,1)} %get-tuple-element.41), kind=kOutput, calls=%fused_computation.51 | convolution fusion | flops 1813118976 | bytes 89653248 | tf_op jit(solution)/shard_map/cpsl,srl->cprs/dot_general | solution.py:86
  208.0 27.7 %slice_bitcast_fusion.16 = (f32[1,12,2,16,96]{3,1,2,4,0:T(8,128)}, f32[1,12,2,16,96]{3,1,2,4,0:T(8,128)}, f32[1,12,2,16,96]{3,1,2,4,0:T(8,128)}, f32[1,12,2,16,9...) fusion(f32[12,2,256,96]{2,0,1,3:T(8,128)} %get-tuple-element.45), kind=kLoop, calls=%fused_computation.75 | loop fusion | bytes 4718592 | tf_op jit(solution)/shard_map/stack | solution.py:95
  277.5 11.5 slice_bitcast_fusion
  370.4 8.1 fusion.76
  378.4 8.1 fusion.74
  386.5 119.3 %all-to-all-done.1 = f32[32,12,2,16,96]{4,3,2,1,0:T(8,128)} async-done(((f32[32,12,2,16,96]{4,3,2,1,0:T(8,128)}), f32[32,12,2,16,96]{4,3,2,1,0:T(8,128)}, u32[]{:S(2)}, u32[]{:S(2)}) %all-to-all-start.1) | async-done | bytes 4718624 | tf_op jit(solution)/shard_map/all_to_all | solution.py:94
  505.9 9.1 copy.168
  525.5 95.4 %multiply_add_fusion = (f32[192,64,3072]{2,1,0:T(8,128)}, f32[192,64,3072]{2,1,0:T(8,128)}) fusion(f32[64,3072]{1,0:T(8,128)} %get-tuple-element.81, f32[192,3072]{1,0:T(8,128)S(1)} %bitcast.169, f32[64,3072]{1,0:T(8,128)} %get-tuple-element.80, f32[192,3072]{1,0:T(8,128)S(1)} %bitcast.168), kind=kLoop, calls=%fused_computation.39 | loop fusion | flops 226492416 | bytes 308281344 | tf_op jit(solution)/shard_map/add | solution.py:32
  621.0 126.1 %fusion.34 = f32[12288,128]{1,0:T(8,128)} fusion(f32[12288,3072]{1,0:T(8,128)} %bitcast.60, f32[3072,128]{1,0:T(8,128)} %fusion.76), kind=kOutput, calls=%fused_computation.93 | convolution fusion | flops 57982058496 | bytes 158859264 | tf_op jit(solution)/shard_map/dot_general | solution.py:35
  747.0 125.4 %convolution_subtract_fusion = f32[12288,128]{1,0:T(8,128)} fusion(f32[12288,128]{1,0:T(8,128)} %fusion.34, f32[12288,3072]{1,0:T(8,128)} %bitcast.61, f32[3072,128]{1,0:T(8,128)S(1)} %copy-done), kind=kOutput, calls=%fused_computation.45 | convolution fusion | flops 57983631360 | bytes 165150720 | tf_op jit(solution)/shard_map/dot_general | solution.py:36
  879.8 9.7 copy.183
  889.5 686.4 %while.10 = (s32[]{:T(128)}, f32[16,8192]{1,0:T(8,128)}, s32[16,16]{1,0:T(8,128)}, f32[16,12,8192]{2,1,0:T(8,128)}, s32[]{:T(128)}, /*index=5*/s32[]{:T(128)}, f32[]{:T(128)}, f32[]{:T(128)}) while((s32[]{:T(128)}, f32[16,8192]{1,0:T(8,128)}, s32[16,16]{1,0:T(8,128)}, f32[16,12,8192]{2,1,0:T(8,128)}, s32[]{:T(128)}, /*index=5*/s32[]{:T(128)}, ...), condition=%wide.region_7.8_spmd, body=%wide.region_0.7_spmd.sunk | while | flops 247610512 | bytes 1840549 | solution.py:103
  896.5 17.6 %custom-call.14 = f32[16,12,12]{2,1,0:T(8,128)S(1)} custom-call(f32[16,12,12]{2,1,0:T(8,128)S(1)} %copy.193), custom_call_target="Cholesky" | custom-call | tf_op jit(solution)/shard_map/while/body/eval_jaxpr/jit(cholesky)/cholesky | solution.py:61
  914.4 14.9 custom-call.15
  939.4 17.6 %custom-call.14 = f32[16,12,12]{2,1,0:T(8,128)S(1)} custom-call(f32[16,12,12]{2,1,0:T(8,128)S(1)} %copy.193), custom_call_target="Cholesky" | custom-call | tf_op jit(solution)/shard_map/while/body/eval_jaxpr/jit(cholesky)/cholesky | solution.py:61
  957.3 14.9 custom-call.15
  982.3 17.6 %custom-call.14 = f32[16,12,12]{2,1,0:T(8,128)S(1)} custom-call(f32[16,12,12]{2,1,0:T(8,128)S(1)} %copy.193), custom_call_target="Cholesky" | custom-call | tf_op jit(solution)/shard_map/while/body/eval_jaxpr/jit(cholesky)/cholesky | solution.py:61
  1000.2 14.9 custom-call.15
  1025.2 17.6 %custom-call.14 = f32[16,12,12]{2,1,0:T(8,128)S(1)} custom-call(f32[16,12,12]{2,1,0:T(8,128)S(1)} %copy.193), custom_call_target="Cholesky" | custom-call | tf_op jit(solution)/shard_map/while/body/eval_jaxpr/jit(cholesky)/cholesky | solution.py:61
  1043.1 14.9 custom-call.15
  1068.1 17.6 %custom-call.14 = f32[16,12,12]{2,1,0:T(8,128)S(1)} custom-call(f32[16,12,12]{2,1,0:T(8,128)S(1)} %copy.193), custom_call_target="Cholesky" | custom-call | tf_op jit(solution)/shard_map/while/body/eval_jaxpr/jit(cholesky)/cholesky | solution.py:61
  1086.0 14.9 custom-call.15
  1111.0 17.6 %custom-call.14 = f32[16,12,12]{2,1,0:T(8,128)S(1)} custom-call(f32[16,12,12]{2,1,0:T(8,128)S(1)} %copy.193), custom_call_target="Cholesky" | custom-call | tf_op jit(solution)/shard_map/while/body/eval_jaxpr/jit(cholesky)/cholesky | solution.py:61
  1128.9 14.9 custom-call.15
  1153.9 17.6 %custom-call.14 = f32[16,12,12]{2,1,0:T(8,128)S(1)} custom-call(f32[16,12,12]{2,1,0:T(8,128)S(1)} %copy.193), custom_call_target="Cholesky" | custom-call | tf_op jit(solution)/shard_map/while/body/eval_jaxpr/jit(cholesky)/cholesky | solution.py:61
  1171.8 14.9 custom-call.15
  1196.8 17.6 %custom-call.14 = f32[16,12,12]{2,1,0:T(8,128)S(1)} custom-call(f32[16,12,12]{2,1,0:T(8,128)S(1)} %copy.193), custom_call_target="Cholesky" | custom-call | tf_op jit(solution)/shard_map/while/body/eval_jaxpr/jit(cholesky)/cholesky | solution.py:61
  1214.7 14.9 custom-call.15
  1239.7 17.6 %custom-call.14 = f32[16,12,12]{2,1,0:T(8,128)S(1)} custom-call(f32[16,12,12]{2,1,0:T(8,128)S(1)} %copy.193), custom_call_target="Cholesky" | custom-call | tf_op jit(solution)/shard_map/while/body/eval_jaxpr/jit(cholesky)/cholesky | solution.py:61
  1257.6 14.9 custom-call.15
  1282.6 17.6 %custom-call.14 = f32[16,12,12]{2,1,0:T(8,128)S(1)} custom-call(f32[16,12,12]{2,1,0:T(8,128)S(1)} %copy.193), custom_call_target="Cholesky" | custom-call | tf_op jit(solution)/shard_map/while/body/eval_jaxpr/jit(cholesky)/cholesky | solution.py:61
  1300.5 14.9 custom-call.15
  1325.5 17.6 %custom-call.14 = f32[16,12,12]{2,1,0:T(8,128)S(1)} custom-call(f32[16,12,12]{2,1,0:T(8,128)S(1)} %copy.193), custom_call_target="Cholesky" | custom-call | tf_op jit(solution)/shard_map/while/body/eval_jaxpr/jit(cholesky)/cholesky | solution.py:61
  1343.4 14.9 custom-call.15
  1368.4 17.6 %custom-call.14 = f32[16,12,12]{2,1,0:T(8,128)S(1)} custom-call(f32[16,12,12]{2,1,0:T(8,128)S(1)} %copy.193), custom_call_target="Cholesky" | custom-call | tf_op jit(solution)/shard_map/while/body/eval_jaxpr/jit(cholesky)/cholesky | solution.py:61
  1386.3 14.9 custom-call.15
  1411.3 17.6 %custom-call.14 = f32[16,12,12]{2,1,0:T(8,128)S(1)} custom-call(f32[16,12,12]{2,1,0:T(8,128)S(1)} %copy.193), custom_call_target="Cholesky" | custom-call | tf_op jit(solution)/shard_map/while/body/eval_jaxpr/jit(cholesky)/cholesky | solution.py:61
  1429.2 14.9 custom-call.15
  1454.2 17.6 %custom-call.14 = f32[16,12,12]{2,1,0:T(8,128)S(1)} custom-call(f32[16,12,12]{2,1,0:T(8,128)S(1)} %copy.193), custom_call_target="Cholesky" | custom-call | tf_op jit(solution)/shard_map/while/body/eval_jaxpr/jit(cholesky)/cholesky | solution.py:61
  1472.1 14.9 custom-call.15
  1497.1 17.6 %custom-call.14 = f32[16,12,12]{2,1,0:T(8,128)S(1)} custom-call(f32[16,12,12]{2,1,0:T(8,128)S(1)} %copy.193), custom_call_target="Cholesky" | custom-call | tf_op jit(solution)/shard_map/while/body/eval_jaxpr/jit(cholesky)/cholesky | solution.py:61
  1514.9 14.9 custom-call.15
  1540.0 17.6 %custom-call.14 = f32[16,12,12]{2,1,0:T(8,128)S(1)} custom-call(f32[16,12,12]{2,1,0:T(8,128)S(1)} %copy.193), custom_call_target="Cholesky" | custom-call | tf_op jit(solution)/shard_map/while/body/eval_jaxpr/jit(cholesky)/cholesky | solution.py:61
  1557.8 14.9 custom-call.15
  (555 shorter events, 322.9 us)
Async XLA Ops:
  11.6 6.0 copy-start.20
  11.6 111.1 %all-to-all-start = ((bf16[3,2,384,1536]{3,0,1,2:T(4,128)(2,1)}), bf16[3,2,384,1536]{3,0,1,2:T(4,128)(2,1)}, u32[]{:S(2)}, u32[]{:S(2)}) async-start(bf16[3,2,384,1536]{3,0,1,2:T(4,128)(2,1)} %copy.131), calls=%async_computation | async-start | bytes 18874368 | tf_op jit(solution)/shard_map/all_to_all | solution.py:82
  289.0 16.4 %copy-start.4 = (f32[1,12,2,16,96]{3,1,2,4,0:T(8,128)S(1)}, f32[1,12,2,16,96]{3,1,2,4,0:T(8,128)}, u32[]{:S(2)}) copy-start(f32[1,12,2,16,96]{3,1,2,4,0:T(8,128)} %get-tuple-element.57) | copy-start | bytes 442372
  289.0 17.8 %copy-start.3 = (f32[1,12,2,16,96]{3,1,2,4,0:T(8,128)S(1)}, f32[1,12,2,16,96]{3,1,2,4,0:T(8,128)}, u32[]{:S(2)}) copy-start(f32[1,12,2,16,96]{3,1,2,4,0:T(8,128)} %get-tuple-element.56) | copy-start | bytes 442372
  306.8 17.7 %copy-start.2 = (f32[1,12,2,16,96]{3,1,2,4,0:T(8,128)S(1)}, f32[1,12,2,16,96]{3,1,2,4,0:T(8,128)}, u32[]{:S(2)}) copy-start(f32[1,12,2,16,96]{3,1,2,4,0:T(8,128)} %get-tuple-element.49) | copy-start | bytes 442372
  308.2 17.8 %copy-start.1 = (f32[1,12,2,16,96]{3,1,2,4,0:T(8,128)S(1)}, f32[1,12,2,16,96]{3,1,2,4,0:T(8,128)}, u32[]{:S(2)}) copy-start(f32[1,12,2,16,96]{3,1,2,4,0:T(8,128)} %get-tuple-element.48) | copy-start | bytes 442372
  325.9 20.4 %copy-start.5 = (f32[1,12,2,16,96]{4,3,2,1,0:T(8,128)S(1)}, f32[1,12,2,16,96]{4,3,2,1,0:T(8,128)}, u32[]{:S(2)}) copy-start(f32[1,12,2,16,96]{4,3,2,1,0:T(8,128)} %copy.149) | copy-start | bytes 442372
  325.9 29.6 %copy-start.11 = (f32[1,12,2,16,96]{4,3,2,1,0:T(8,128)S(1)}, f32[1,12,2,16,96]{4,3,2,1,0:T(8,128)}, u32[]{:S(2)}) copy-start(f32[1,12,2,16,96]{4,3,2,1,0:T(8,128)} %copy.161) | copy-start | bytes 442372
  325.9 30.3 %copy-start.10 = (f32[1,12,2,16,96]{4,3,2,1,0:T(8,128)S(1)}, f32[1,12,2,16,96]{4,3,2,1,0:T(8,128)}, u32[]{:S(2)}) copy-start(f32[1,12,2,16,96]{4,3,2,1,0:T(8,128)} %copy.162) | copy-start | bytes 442372
  325.9 31.0 %copy-start.9 = (f32[1,12,2,16,96]{4,3,2,1,0:T(8,128)S(1)}, f32[1,12,2,16,96]{4,3,2,1,0:T(8,128)}, u32[]{:S(2)}) copy-start(f32[1,12,2,16,96]{4,3,2,1,0:T(8,128)} %copy.163) | copy-start | bytes 442372
  325.9 31.7 %copy-start.8 = (f32[1,12,2,16,96]{4,3,2,1,0:T(8,128)S(1)}, f32[1,12,2,16,96]{4,3,2,1,0:T(8,128)}, u32[]{:S(2)}) copy-start(f32[1,12,2,16,96]{4,3,2,1,0:T(8,128)} %copy.164) | copy-start | bytes 442372
  325.9 32.4 %copy-start.7 = (f32[1,12,2,16,96]{4,3,2,1,0:T(8,128)S(1)}, f32[1,12,2,16,96]{4,3,2,1,0:T(8,128)}, u32[]{:S(2)}) copy-start(f32[1,12,2,16,96]{4,3,2,1,0:T(8,128)} %copy.165) | copy-start | bytes 442372
  325.9 33.1 %copy-start.6 = (f32[1,12,2,16,96]{4,3,2,1,0:T(8,128)S(1)}, f32[1,12,2,16,96]{4,3,2,1,0:T(8,128)}, u32[]{:S(2)}) copy-start(f32[1,12,2,16,96]{4,3,2,1,0:T(8,128)} %copy.166) | copy-start | bytes 442372
  326.7 23.3 %copy-start.19 = (f32[1,12,2,16,96]{4,3,2,1,0:T(8,128)S(1)}, f32[1,12,2,16,96]{4,3,2,1,0:T(8,128)}, u32[]{:S(2)}) copy-start(f32[1,12,2,16,96]{4,3,2,1,0:T(8,128)} %copy.153) | copy-start | bytes 442372
  326.7 24.0 %copy-start.18 = (f32[1,12,2,16,96]{4,3,2,1,0:T(8,128)S(1)}, f32[1,12,2,16,96]{4,3,2,1,0:T(8,128)}, u32[]{:S(2)}) copy-start(f32[1,12,2,16,96]{4,3,2,1,0:T(8,128)} %copy.154) | copy-start | bytes 442372
  326.7 24.7 %copy-start.17 = (f32[1,12,2,16,96]{4,3,2,1,0:T(8,128)S(1)}, f32[1,12,2,16,96]{4,3,2,1,0:T(8,128)}, u32[]{:S(2)}) copy-start(f32[1,12,2,16,96]{4,3,2,1,0:T(8,128)} %copy.155) | copy-start | bytes 442372
  326.7 25.3 %copy-start.16 = (f32[1,12,2,16,96]{4,3,2,1,0:T(8,128)S(1)}, f32[1,12,2,16,96]{4,3,2,1,0:T(8,128)}, u32[]{:S(2)}) copy-start(f32[1,12,2,16,96]{4,3,2,1,0:T(8,128)} %copy.156) | copy-start | bytes 442372
  326.7 26.0 %copy-start.15 = (f32[1,12,2,16,96]{4,3,2,1,0:T(8,128)S(1)}, f32[1,12,2,16,96]{4,3,2,1,0:T(8,128)}, u32[]{:S(2)}) copy-start(f32[1,12,2,16,96]{4,3,2,1,0:T(8,128)} %copy.157) | copy-start | bytes 442372
  326.7 26.7 %copy-start.14 = (f32[1,12,2,16,96]{4,3,2,1,0:T(8,128)S(1)}, f32[1,12,2,16,96]{4,3,2,1,0:T(8,128)}, u32[]{:S(2)}) copy-start(f32[1,12,2,16,96]{4,3,2,1,0:T(8,128)} %copy.158) | copy-start | bytes 442372
  326.7 27.4 %copy-start.13 = (f32[1,12,2,16,96]{4,3,2,1,0:T(8,128)S(1)}, f32[1,12,2,16,96]{4,3,2,1,0:T(8,128)}, u32[]{:S(2)}) copy-start(f32[1,12,2,16,96]{4,3,2,1,0:T(8,128)} %copy.159) | copy-start | bytes 442372
  326.7 28.1 %copy-start.12 = (f32[1,12,2,16,96]{4,3,2,1,0:T(8,128)S(1)}, f32[1,12,2,16,96]{4,3,2,1,0:T(8,128)}, u32[]{:S(2)}) copy-start(f32[1,12,2,16,96]{4,3,2,1,0:T(8,128)} %copy.160) | copy-start | bytes 442372
  360.4 145.5 %all-to-all-start.1 = ((f32[32,12,2,16,96]{4,3,2,1,0:T(8,128)}), f32[32,12,2,16,96]{4,3,2,1,0:T(8,128)}, u32[]{:S(2)}, u32[]{:S(2)}) async-start(f32[32,12,2,16,96]{4,3,2,1,0:T(8,128)} %constant_dynamic-update-slice_fusion), calls=%async_computation.1 | async-start | bytes 12582912 | tf_op jit(solution)/shard_map/all_to_all | solution.py:94
  620.9 126.1 %copy-start = (f32[3072,128]{1,0:T(8,128)S(1)}, f32[3072,128]{1,0:T(8,128)}, u32[]{:S(2)}) copy-start(f32[3072,128]{1,0:T(8,128)} %fusion.74) | copy-start | bytes 4718596
